TPU v7x, 512 devices: a whole 4x4x16 slice. The times are simulated.
512 devices in a mesh: dp: 4 (over x), ctx: 32 (over z, core), tp: 4 (over y).
Axes of the slice: x: 4, y: 4, z: 16, core: 2. Of those that a mesh axis runs over, the one named last changes fastest.
Arguments:
- inputs: bfloat16 [4, 4096, 8192], P('dp', 'ctx', 'tp'), may hold values from -6 to 6
- grad_out: bfloat16 [4, 4096, 8192], P('dp', 'ctx', 'tp'), may hold values from -6 to 6
- input_map: bfloat16 [4, 4096, 128], P('dp', 'ctx'), may hold values from -0.5 to 0.5
- output_map: bfloat16 [4, 4096, 128], P('dp', 'ctx'), may hold values from -0.25 to 0.25
- step_size: float32 [4, 128, 4096], P('dp', 'tp', 'ctx'), may hold values from 0.3 to 1.5
- log_decay: float32 [4, 128, 4096], P('dp', 'tp', 'ctx'), may hold values from -2 to 0
- skip_gain: float32 [128], P('tp'), may hold values from 0.5 to 1.5
Outputs:
- mixed: bfloat16 [4, 4096, 8192], P('dp', 'ctx', 'tp')
- grad_inputs: bfloat16 [4, 4096, 8192], P('dp', 'ctx', 'tp')
- grad_step: float32 [4, 128, 4096], P('dp', 'tp', 'ctx')
- grad_decay: float32 [4, 128, 4096], P('dp', 'tp', 'ctx')
- grad_input_map: float32 [4, 4096, 128], P('dp', ('ctx', 'tp'))
- grad_output_map: float32 [4, 4096, 128], P('dp', ('ctx', 'tp'))
- grad_skip: float32 [128], P('tp')
All inputs are finite; a program needn't handle non-finite values.
Results may differ from a plain program's by a relative error of at most 0.0011.
Values sent between devices are 32-bit elements; how exact they have to be, the bound alone decides.
No kernel may reach another device: no remote copies, remote signals or barrier semaphores. Data moves between devices by JAX's collectives and lax.ppermute only.
A program may use at most 192 MiB of HBM per device.

v0:
```python
import math
import jax
import jax.numpy as jnp
from jax import lax
from jax.sharding import PartitionSpec as P

precise = lax.Precision.HIGHEST


def entering(part, axis, combine, identity, reverse):
    count = lax.axis_size(axis)
    place = lax.axis_index(axis)
    ahead = count - 1 - place if reverse else place
    gathered = jax.tree.map(lambda a: lax.all_gather(a, axis), part)
    state = jax.tree.map(lambda a, e: jnp.zeros_like(a) + jnp.asarray(e, a.dtype), part, identity)

    def one(hop, state):
        source = count - 1 - hop if reverse else hop
        return combine(
            state, jax.tree.map(lambda a: lax.dynamic_index_in_dim(a, source, 0, False), gathered)
        )

    return lax.fori_loop(0, ahead, one, state)


def combine_pair(earlier, later_part):
    return (earlier[0] * later_part[0], later_part[0][..., None, None] * earlier[1] + later_part[1])


def block_forward(values, in_map, out_map, steps, logs):
    cumulative = jnp.cumsum(logs, axis=-1)
    length = cumulative.shape[-1]
    row_ids = lax.broadcasted_iota(jnp.int32, (length, length), 0)
    column_ids = lax.broadcasted_iota(jnp.int32, (length, length), 1)
    causal = row_ids >= column_ids
    spread = cumulative[..., :, None] - cumulative[..., None, :]
    decays = jnp.where(causal, jnp.exp(jnp.where(causal, spread, 0.0)), 0.0)
    affinity = jnp.einsum("btn,bsn->bts", out_map, in_map, precision=precise)
    mixing = decays * affinity[:, None]
    scaled = values * jnp.transpose(steps, (0, 2, 1))[..., None]
    remain = jnp.exp(cumulative[..., -1:] - cumulative)
    weighted = remain[..., None] * in_map[:, None]
    local_state = jnp.einsum("bshp,bhsn->bhpn", scaled, weighted, precision=precise)
    through = jnp.exp(cumulative[..., -1])
    return (cumulative, decays, mixing, scaled, remain, local_state, through)


def block_output(values, out_map, skip_gain, cumulative, mixing, scaled, incoming):
    within = jnp.einsum("bhts,bshp->bthp", mixing, scaled, precision=precise)
    carried = jnp.einsum("bhpn,btn->bthp", incoming, out_map, precision=precise)
    carried = carried * jnp.transpose(jnp.exp(cumulative), (0, 2, 1))[..., None]
    return (within + carried + skip_gain[:, None] * values, carried)


def block_source(cotangent, out_map, cumulative):
    weighted = jnp.exp(cumulative)[..., None] * out_map[:, None]
    return jnp.einsum("bshp,bhsn->bhpn", cotangent, weighted, precision=precise)


def block_backward(
    values,
    cotangent,
    in_map,
    out_map,
    steps,
    skip_gain,
    cumulative,
    decays,
    mixing,
    scaled,
    remain,
    local_state,
    through,
    incoming,
    carried,
    arriving,
):
    remain_col = jnp.transpose(remain, (0, 2, 1))[..., None]
    starts = jnp.transpose(jnp.exp(cumulative), (0, 2, 1))[..., None]
    steps_col = jnp.transpose(steps, (0, 2, 1))[..., None]
    from_later = jnp.einsum("bhpn,btn->bthp", arriving, in_map, precision=precise)
    state_grad = (
        jnp.einsum("bhst,bshp->bthp", mixing, cotangent, precision=precise)
        + remain_col * from_later
    )
    grad_values = steps_col * state_grad + skip_gain[:, None] * cotangent
    grad_steps = jnp.transpose(jnp.sum(values * state_grad, axis=-1), (0, 2, 1))
    products = jnp.einsum("bthp,bshp->bhts", cotangent, scaled, precision=precise)
    summed = jnp.sum(decays * products, axis=1)
    grad_in_map = jnp.einsum("bts,btn->bsn", summed, out_map, precision=precise) + jnp.einsum(
        "bthp,bhpn->btn", scaled * remain_col, arriving, precision=precise
    )
    grad_out_map = jnp.einsum("bts,bsn->btn", summed, in_map, precision=precise) + jnp.einsum(
        "bthp,bhpn->btn", cotangent * starts, incoming, precision=precise
    )
    paired = mixing * products
    change = jnp.sum(paired, axis=-1) - jnp.sum(paired, axis=-2)
    change = change + jnp.transpose(jnp.sum(cotangent * carried, axis=-1), (0, 2, 1))
    change = change - remain * jnp.transpose(jnp.sum(scaled * from_later, axis=-1), (0, 2, 1))
    final_edge = jnp.sum(arriving * local_state, axis=(2, 3)) + through * jnp.sum(
        arriving * incoming, axis=(2, 3)
    )
    length = change.shape[-1]
    ending = lax.broadcasted_iota(jnp.int32, (length,), 0) == length - 1
    change = change + jnp.where(ending, final_edge[..., None], 0.0)
    grad_logs = lax.cumsum(change, axis=2, reverse=True)
    skip_part = jnp.sum(cotangent * values, axis=(0, 1, 3))
    return (grad_values, grad_steps, grad_in_map, grad_out_map, grad_logs, skip_part)


def shards(inputs, grad_out, input_map, output_map, step_size, log_decay, skip_gain):
    sequences, length, features = inputs.shape
    heads = step_size.shape[1]
    per_head = features // heads
    values = inputs.reshape(sequences, length, heads, per_head).astype(jnp.float32)
    cotangent = grad_out.reshape(sequences, length, heads, per_head).astype(jnp.float32)
    in_map = input_map.astype(jnp.float32)
    out_map = output_map.astype(jnp.float32)
    cumulative, decays, mixing, scaled, remain, local_state, through = block_forward(
        values, in_map, out_map, step_size, log_decay
    )
    source = block_source(cotangent, out_map, cumulative)
    neutral = (jnp.ones_like(through), jnp.zeros_like(local_state))
    ahead = entering((through, local_state), "ctx", combine_pair, neutral, False)
    behind = entering((through, source), "ctx", combine_pair, neutral, True)
    incoming = ahead[1]
    arriving = behind[1]
    mixed, carried = block_output(values, out_map, skip_gain, cumulative, mixing, scaled, incoming)
    results = block_backward(
        values,
        cotangent,
        in_map,
        out_map,
        step_size,
        skip_gain,
        cumulative,
        decays,
        mixing,
        scaled,
        remain,
        local_state,
        through,
        incoming,
        carried,
        arriving,
    )
    grad_values, grad_steps, grad_in_part, grad_out_part, grad_logs, skip_part = results
    grad_in_map, grad_out_map = (
        lax.psum_scatter(grad_in_part, "tp", scatter_dimension=1, tiled=True),
        lax.psum_scatter(grad_out_part, "tp", scatter_dimension=1, tiled=True),
    )
    skip_total = lax.psum(skip_part, ("dp", "ctx"))
    factor = 1.0 / math.sqrt(
        sequences * lax.axis_size("dp") * length * lax.axis_size("ctx") * per_head
    )
    mixed_out = mixed.reshape(sequences, length, features).astype(jnp.bfloat16)
    grad_inputs = grad_values.reshape(sequences, length, features).astype(jnp.bfloat16)
    return (
        mixed_out,
        grad_inputs,
        grad_steps,
        grad_logs,
        grad_in_map,
        grad_out_map,
        skip_total * factor,
    )


def solution(mesh):
    in_specs = (
        P("dp", "ctx", "tp"),
        P("dp", "ctx", "tp"),
        P("dp", "ctx", None),
        P("dp", "ctx", None),
        P("dp", "tp", "ctx"),
        P("dp", "tp", "ctx"),
        P("tp"),
    )
    out_specs = (
        P("dp", "ctx", "tp"),
        P("dp", "ctx", "tp"),
        P("dp", "tp", "ctx"),
        P("dp", "tp", "ctx"),
        P("dp", ("ctx", "tp"), None),
        P("dp", ("ctx", "tp"), None),
        P("tp"),
    )
    return jax.shard_map(shards, mesh=mesh, in_specs=in_specs, out_specs=out_specs, check_vma=False)
```

profile of v0, /device:TPU:2, one launch (start us, length us, event | category | flops | bytes accessed | tf_op | source)
XLA Modules:
  0.0 737.4 jit_solution(14283848565593800011)
XLA Ops:
  9.9 3.2 fusion.3
  13.5 2.4 fusion.16
  16.1 36.1 %all-gather = f32[32,32,1]{1,2,0:T(1,128)S(1)} all-gather(f32[1,32,1]{1,2,0:T(1,128)S(1)} %exp.61), channel_id=2, replica_groups=mesh['dp'=4,'ctx'=32,'tp'=4] {'ctx'}, dimensions={0}, use_global_device_ids=true | all-gather | bytes 4224 | tf_op jit(solution)/shard_map/all_gather | solution.py:14
  52.3 3.1 fusion.20
  55.4 153.7 %all-gather.6.cloned.1.call-done = f32[1024,64,128]{2,1,0:T(8,128)} async-done(((f32[32,64,128]{2,1,0:T(8,128)}), f32[1024,64,128]{2,1,0:T(8,128)}) %all-gather.6.cloned.1.call-update) | async-done | bytes 33554448 | tf_op jit(solution)/shard_map/all_gather | solution.py:14
  209.2 191.1 %all-gather.8.cloned.1.call-done = f32[1024,64,128]{2,1,0:T(8,128)} async-done(((f32[32,64,128]{2,1,0:T(8,128)}), f32[1024,64,128]{2,1,0:T(8,128)}) %all-gather.8.cloned.1.call-update) | async-done | bytes 33554448 | tf_op jit(solution)/shard_map/all_gather | solution.py:14
  400.4 46.3 %while.27 = (s32[]{:T(128)}, f32[1,32,64,128]{3,2,1,0:T(8,128)S(1)}, s32[]{:T(128)}, f32[32,1,32]{2,1,0:T(1,128)S(1)}, f32[32,1,32,64,128]{4,3,2,1,0:T(8,128)}, ...) while((s32[]{:T(128)}, f32[1,32,64,128]{3,2,1,0:T(8,128)S(1)}, s32[]{:T(128)}, f32[32,1,32]{2,1,0:T(1,128)S(1)}, ...), condition=%wide.region_4.5_spmd, body=%wide.region_3.4_spmd.sunk | while | flops 524294 | bytes 3146259 | solution.py:23
  400.4 1.4 bitcast_add_fusion.6
  401.9 1.4 bitcast_add_fusion.6
  403.4 1.4 bitcast_add_fusion.6
  404.9 1.4 bitcast_add_fusion.6
  406.4 1.4 bitcast_add_fusion.6
  407.9 1.4 bitcast_add_fusion.6
  409.4 1.4 bitcast_add_fusion.6
  410.9 1.4 bitcast_add_fusion.6
  412.4 1.4 bitcast_add_fusion.6
  413.9 1.4 bitcast_add_fusion.6
  415.4 1.4 bitcast_add_fusion.6
  416.9 1.4 bitcast_add_fusion.6
  418.3 1.4 bitcast_add_fusion.6
  419.8 1.4 bitcast_add_fusion.6
  434.8 1.4 bitcast_add_fusion.6
  443.8 1.4 bitcast_add_fusion.6
  446.7 1.6 multiply_reduce_fusion.2
  449.4 1.6 multiply_reduce_fusion.3
  452.4 1.9 convolution_bitcast_fusion.2
  455.5 3.8 fusion.31
  459.3 3.2 multiply_reduce_fusion.4
  462.4 1.9 convolution_bitcast_fusion.3
  466.5 208.1 %psum.7 = f32[32]{0:T(128)S(1)} all-reduce(f32[32]{0:T(128)S(1)} %reduce_sum.113), channel_id=1, replica_groups=mesh['dp'=4,'ctx'=32,'tp'=4] {'dp','ctx'}, use_global_device_ids=true, to_apply=%region_18.19 | all-reduce | flops 32 | bytes 256 | tf_op jit(solution)/shard_map/psum | solution.py:152
  675.4 1.8 reduce_window_sum.22
  677.8 53.1 %reduce-scatter.3.cloned.1.call-done = f32[1,32,128]{2,1,0:T(8,128)} async-done(((f32[1,128,128]{2,1,0:T(8,128)}), f32[1,32,128]{2,1,0:T(8,128)}) %reduce-scatter.3.cloned.1.call-update) | async-done | bytes 16400 | tf_op jit(solution)/shard_map/reduce_scatter | solution.py:149
  (109 shorter events, 32.5 us)
Async XLA Ops:
  7.2 2.7 copy-start.8
  7.2 2.8 copy-start.11
  7.2 201.8 %all-gather.6.cloned.1.call-start = ((), (), s32[]{:S(2)}) async-start(), calls=%async_computation.4 | async-start | bytes 34603008 | tf_op jit(solution)/shard_map/all_gather | solution.py:14
  9.8 3.3 copy-start.4
  9.8 3.4 copy-start.10
  9.9 3.6 copy-start.9
  13.1 387.1 %all-gather.8.cloned.1.call-start = ((), (), s32[]{:S(2)}) async-start(), calls=%async_computation.5 | async-start | bytes 34603008 | tf_op jit(solution)/shard_map/all_gather | solution.py:14
  13.5 41.9 %copy-start.1 = (bf16[1,128,2048]{1,2,0:T(8,128)(2,1)}, bf16[1,128,2048]{1,2,0:T(8,128)(2,1)S(1)}, u32[]{:S(2)}) copy-start(bf16[1,128,2048]{1,2,0:T(8,128)(2,1)S(1)} %copy.84) | copy-start | bytes 1572868
  16.0 661.8 %reduce-scatter.5.cloned.1.call-start = ((), (), s32[]{:S(2)}) async-start(), calls=%async_computation.3 | async-start | bytes 81920 | tf_op jit(solution)/shard_map/reduce_scatter | solution.py:150
  446.7 1.6 copy-start
  448.3 1.0 copy-start.2
  449.4 1.7 copy-start.5
  451.1 4.3 copy-start.12
  455.2 275.7 %reduce-scatter.3.cloned.1.call-start = ((), (), s32[]{:S(2)}) async-start(), calls=%async_computation.2 | async-start | bytes 81920 | tf_op jit(solution)/shard_map/reduce_scatter | solution.py:149
  455.4 3.8 copy-start.3
  455.5 3.8 copy-start.7
  459.3 3.2 copy-start.6
Sparse Core Ops, SparseCore 0:
  13.3 195.7 all-gather.5
  211.1 189.0 all-gather.7
  455.3 18.9 reduce-scatter.4
  675.5 55.2 reduce-scatter.2
where the time goes:
time: 739 us; the launch traced here: 737 us
  waiting for transfers between devices  398 us (54%)
  blocking collectives  244 us (33%)
  other arithmetic  50.2 us (7%)
  matrix products  24.4 us (3%)
  between operations  14.1 us (2%)
    all_gather x2, waiting for transfers between devices, entering(): gathered = jax.tree.map(lambda a: lax.all_gather(a, axis), part)  345 us
    psum x1, blocking collectives, shards(): skip_total = lax.psum(skip_part, ('dp', 'ctx'))  208 us
    reduce_scatter x1, waiting for transfers between devices, shards(): lax.psum_scatter(grad_in_part, 'tp', scatter_dimension=1, tiled=True)  53.1 us
    add x31, other arithmetic, combine_pair(): later_part[0][..., None, None] * earlier[1] + later_part[1]  44.9 us
    all_gather x1, blocking collectives, entering(): gathered = jax.tree.map(lambda a: lax.all_gather(a, axis), part)  36.1 us
  transfers between devices with their start and end apart: 4, of which 3 were waited for; matrix products, arithmetic and copies ran while one was open for 3% of the time, Pallas kernels for 0%

commit v1 on v0

--- a/solution.py
+++ b/solution.py
@@ -149,7 +149,7 @@
         lax.psum_scatter(grad_in_part, "tp", scatter_dimension=1, tiled=True),
         lax.psum_scatter(grad_out_part, "tp", scatter_dimension=1, tiled=True),
     )
-    skip_total = lax.psum(skip_part, ("dp", "ctx"))
+    skip_total = lax.psum(lax.psum(skip_part, "ctx"), "dp")
     factor = 1.0 / math.sqrt(
         sequences * lax.axis_size("dp") * length * lax.axis_size("ctx") * per_head
     )

time: 739 us -> 549 us (0.74)
  blocking collectives: 244 us -> 90.4 us
  waiting for transfers between devices: 398 us -> 361 us
    psum x1 -> x2, blocking collectives: 208 us -> 54.4 us  [shards(): skip_total = lax.psum(lax.psum(skip_part, 'ctx'), 'dp')]
    reduce_scatter x1, waiting for transfers between devices: 53.1 us -> 16.6 us  [shards(): lax.psum_scatter(grad_in_part, 'tp', scatter_dimension=1, tiled=True)]
  transfers between devices with their start and end apart: 4 -> 4, of which waited for: 3 -> 3; matrix products, arithmetic and copies ran while one was open for 3% -> 4% of each run, Pallas kernels for 0% -> 0%
where the time goes in v1:
time: 549 us; the launch traced here: 547 us
  waiting for transfers between devices  361 us (66%)
  blocking collectives  90.4 us (16%)
  other arithmetic  50.2 us (9%)
  matrix products  24.4 us (4%)
  between operations  14.1 us (3%)
    all_gather x2, waiting for transfers between devices, entering(): gathered = jax.tree.map(lambda a: lax.all_gather(a, axis), part)  345 us
    psum x2, blocking collectives, shards(): skip_total = lax.psum(lax.psum(skip_part, 'ctx'), 'dp')  54.4 us
    add x31, other arithmetic, combine_pair(): later_part[0][..., None, None] * earlier[1] + later_part[1]  44.9 us
    all_gather x1, blocking collectives, entering(): gathered = jax.tree.map(lambda a: lax.all_gather(a, axis), part)  36.1 us
    reduce_scatter x1, waiting for transfers between devices, shards(): lax.psum_scatter(grad_in_part, 'tp', scatter_dimension=1, tiled=True)  16.6 us
  transfers between devices with their start and end apart: 4, of which 3 were waited for; matrix products, arithmetic and copies ran while one was open for 4% of the time, Pallas kernels for 0%

profile of v1, /device:TPU:2, one launch (start us, length us, event | category | flops | bytes accessed | tf_op | source)
XLA Modules:
  0.0 547.2 jit_solution(9494248271524751189)
XLA Ops:
  9.9 3.2 fusion.3
  13.5 2.4 fusion.16
  16.1 36.1 %all-gather = f32[32,32,1]{1,2,0:T(1,128)S(1)} all-gather(f32[1,32,1]{1,2,0:T(1,128)S(1)} %exp.61), channel_id=2, replica_groups=mesh['dp'=4,'ctx'=32,'tp'=4] {'ctx'}, dimensions={0}, use_global_device_ids=true | all-gather | bytes 4224 | tf_op jit(solution)/shard_map/all_gather | solution.py:14
  52.3 3.1 fusion.20
  55.4 153.7 %all-gather.6.cloned.1.call-done = f32[1024,64,128]{2,1,0:T(8,128)} async-done(((f32[32,64,128]{2,1,0:T(8,128)}), f32[1024,64,128]{2,1,0:T(8,128)}) %all-gather.6.cloned.1.call-update) | async-done | bytes 33554448 | tf_op jit(solution)/shard_map/all_gather | solution.py:14
  209.2 191.1 %all-gather.8.cloned.1.call-done = f32[1024,64,128]{2,1,0:T(8,128)} async-done(((f32[32,64,128]{2,1,0:T(8,128)}), f32[1024,64,128]{2,1,0:T(8,128)}) %all-gather.8.cloned.1.call-update) | async-done | bytes 33554448 | tf_op jit(solution)/shard_map/all_gather | solution.py:14
  400.4 46.3 %while.27 = (s32[]{:T(128)}, f32[1,32,64,128]{3,2,1,0:T(8,128)S(1)}, s32[]{:T(128)}, f32[32,1,32]{2,1,0:T(1,128)S(1)}, f32[32,1,32,64,128]{4,3,2,1,0:T(8,128)}, ...) while((s32[]{:T(128)}, f32[1,32,64,128]{3,2,1,0:T(8,128)S(1)}, s32[]{:T(128)}, f32[32,1,32]{2,1,0:T(1,128)S(1)}, ...), condition=%wide.region_4.5_spmd, body=%wide.region_3.4_spmd.sunk | while | flops 524294 | bytes 3146259 | solution.py:23
  400.4 1.4 bitcast_add_fusion.6
  401.9 1.4 bitcast_add_fusion.6
  403.4 1.4 bitcast_add_fusion.6
  404.9 1.4 bitcast_add_fusion.6
  406.4 1.4 bitcast_add_fusion.6
  407.9 1.4 bitcast_add_fusion.6
  409.4 1.4 bitcast_add_fusion.6
  410.9 1.4 bitcast_add_fusion.6
  412.4 1.4 bitcast_add_fusion.6
  413.9 1.4 bitcast_add_fusion.6
  415.4 1.4 bitcast_add_fusion.6
  416.9 1.4 bitcast_add_fusion.6
  418.3 1.4 bitcast_add_fusion.6
  434.8 1.4 bitcast_add_fusion.6
  443.8 1.4 bitcast_add_fusion.6
  446.7 1.6 multiply_reduce_fusion.2
  449.4 1.6 multiply_reduce_fusion.3
  452.4 1.9 convolution_bitcast_fusion.2
  455.5 3.8 fusion.31
  459.3 3.2 multiply_reduce_fusion.4
  462.4 1.9 convolution_bitcast_fusion.3
  466.5 45.8 %psum.14 = f32[32]{0:T(128)S(1)} all-reduce(f32[32]{0:T(128)S(1)} %reduce_sum.113), channel_id=1, replica_groups=mesh['dp'=4,'ctx'=32,'tp'=4] {'ctx'}, use_global_device_ids=true, to_apply=%region_18.19 | all-reduce | flops 32 | bytes 256 | tf_op jit(solution)/shard_map/psum | solution.py:152
  512.3 8.6 %psum.15 = f32[32]{0:T(128)S(1)} all-reduce(f32[32]{0:T(128)S(1)} %psum.14), channel_id=1, replica_groups=mesh['dp'=4,'ctx'=32,'tp'=4] {'dp'}, use_global_device_ids=true, to_apply=%region_19.20 | all-reduce | flops 32 | bytes 256 | tf_op jit(solution)/shard_map/psum | solution.py:152
  521.7 1.8 reduce_window_sum.22
  524.1 16.6 %reduce-scatter.3.cloned.1.call-done = f32[1,32,128]{2,1,0:T(8,128)} async-done(((f32[1,128,128]{2,1,0:T(8,128)}), f32[1,32,128]{2,1,0:T(8,128)}) %reduce-scatter.3.cloned.1.call-update) | async-done | bytes 16400 | tf_op jit(solution)/shard_map/reduce_scatter | solution.py:149
  (110 shorter events, 33.9 us)
Async XLA Ops:
  7.2 2.7 copy-start.8
  7.2 2.8 copy-start.11
  7.2 201.8 %all-gather.6.cloned.1.call-start = ((), (), s32[]{:S(2)}) async-start(), calls=%async_computation.4 | async-start | bytes 34603008 | tf_op jit(solution)/shard_map/all_gather | solution.py:14
  9.8 3.3 copy-start.4
  9.8 3.4 copy-start.10
  9.9 3.6 copy-start.9
  13.1 387.1 %all-gather.8.cloned.1.call-start = ((), (), s32[]{:S(2)}) async-start(), calls=%async_computation.5 | async-start | bytes 34603008 | tf_op jit(solution)/shard_map/all_gather | solution.py:14
  13.5 41.9 %copy-start.1 = (bf16[1,128,2048]{1,2,0:T(8,128)(2,1)}, bf16[1,128,2048]{1,2,0:T(8,128)(2,1)S(1)}, u32[]{:S(2)}) copy-start(bf16[1,128,2048]{1,2,0:T(8,128)(2,1)S(1)} %copy.84) | copy-start | bytes 1572868
  16.0 508.1 %reduce-scatter.5.cloned.1.call-start = ((), (), s32[]{:S(2)}) async-start(), calls=%async_computation.3 | async-start | bytes 81920 | tf_op jit(solution)/shard_map/reduce_scatter | solution.py:150
  446.7 1.6 copy-start
  448.3 1.0 copy-start.2
  449.4 1.7 copy-start.5
  451.1 4.3 copy-start.12
  455.2 85.5 %reduce-scatter.3.cloned.1.call-start = ((), (), s32[]{:S(2)}) async-start(), calls=%async_computation.2 | async-start | bytes 81920 | tf_op jit(solution)/shard_map/reduce_scatter | solution.py:149
  455.4 3.8 copy-start.3
  455.5 3.8 copy-start.7
  459.3 3.2 copy-start.6
Sparse Core Ops, SparseCore 0:
  13.3 195.7 all-gather.5
  211.1 189.0 all-gather.7
  455.3 18.9 reduce-scatter.4
  521.8 18.7 reduce-scatter.2

commit v2 on v0

--- a/solution.py
+++ b/solution.py
@@ -149,7 +149,7 @@
         lax.psum_scatter(grad_in_part, "tp", scatter_dimension=1, tiled=True),
         lax.psum_scatter(grad_out_part, "tp", scatter_dimension=1, tiled=True),
     )
-    skip_total = lax.psum(skip_part, ("dp", "ctx"))
+    skip_total = jnp.sum(lax.all_gather(skip_part, ("dp", "ctx")), axis=0)
     factor = 1.0 / math.sqrt(
         sequences * lax.axis_size("dp") * length * lax.axis_size("ctx") * per_head
     )

time: 739 us -> 985 us (1.33)
  blocking collectives: 244 us -> 456 us
  waiting for transfers between devices: 398 us -> 428 us
    unnamed x0 -> x1, blocking collectives: none -> 420 us
    psum x1 -> x0, blocking collectives: 208 us -> none  [shards(): skip_total = lax.psum(skip_part, ('dp', 'ctx'))]
    reduce_scatter x1, waiting for transfers between devices: 53.1 us -> 85 us  [shards(): lax.psum_scatter(grad_in_part, 'tp', scatter_dimension=1, tiled=True)]
  transfers between devices with their start and end apart: 4 -> 4, of which waited for: 3 -> 3; matrix products, arithmetic and copies ran while one was open for 3% -> 2% of each run, Pallas kernels for 0% -> 0%
where the time goes in v2:
time: 985 us; the launch traced here: 983 us
  blocking collectives  456 us (46%)
  waiting for transfers between devices  428 us (43%)
  other arithmetic  50.3 us (5%)
  matrix products  25.8 us (3%)
  between operations  14.7 us (1%)
    unnamed x1, blocking collectives  420 us
    all_gather x2, waiting for transfers between devices, entering(): gathered = jax.tree.map(lambda a: lax.all_gather(a, axis), part)  343 us
    reduce_scatter x1, waiting for transfers between devices, shards(): lax.psum_scatter(grad_in_part, 'tp', scatter_dimension=1, tiled=True)  85 us
    add x31, other arithmetic, combine_pair(): later_part[0][..., None, None] * earlier[1] + later_part[1]  44.9 us
    all_gather x1, blocking collectives, entering(): gathered = jax.tree.map(lambda a: lax.all_gather(a, axis), part)  36.1 us
  transfers between devices with their start and end apart: 4, of which 3 were waited for; matrix products, arithmetic and copies ran while one was open for 2% of the time, Pallas kernels for 0%

profile of v2, /device:TPU:2, one launch (start us, length us, event | category | flops | bytes accessed | tf_op | source)
XLA Modules:
  0.0 983.3 jit_solution(3786408761635333082)
XLA Ops:
  9.9 3.2 fusion.3
  13.5 2.4 fusion.16
  18.0 36.1 %all-gather = f32[32,32,1]{1,2,0:T(1,128)S(1)} all-gather(f32[1,32,1]{1,2,0:T(1,128)S(1)} %exp.61), channel_id=2, replica_groups=mesh['dp'=4,'ctx'=32,'tp'=4] {'ctx'}, dimensions={0}, use_global_device_ids=true | all-gather | bytes 4224 | tf_op jit(solution)/shard_map/all_gather | solution.py:14
  54.2 3.1 fusion.20
  57.3 151.7 %all-gather.7.cloned.1.call-done = f32[1024,64,128]{2,1,0:T(8,128)} async-done(((f32[32,64,128]{2,1,0:T(8,128)}), f32[1024,64,128]{2,1,0:T(8,128)}) %all-gather.7.cloned.1.call-update) | async-done | bytes 33554448 | tf_op jit(solution)/shard_map/all_gather | solution.py:14
  209.2 191.1 %all-gather.9.cloned.1.call-done = f32[1024,64,128]{2,1,0:T(8,128)} async-done(((f32[32,64,128]{2,1,0:T(8,128)}), f32[1024,64,128]{2,1,0:T(8,128)}) %all-gather.9.cloned.1.call-update) | async-done | bytes 33554448 | tf_op jit(solution)/shard_map/all_gather | solution.py:14
  400.4 46.3 %while.27 = (s32[]{:T(128)}, f32[1,32,64,128]{3,2,1,0:T(8,128)S(1)}, s32[]{:T(128)}, f32[32,1,32]{2,1,0:T(1,128)S(1)}, f32[32,1,32,64,128]{4,3,2,1,0:T(8,128)}, ...) while((s32[]{:T(128)}, f32[1,32,64,128]{3,2,1,0:T(8,128)S(1)}, s32[]{:T(128)}, f32[32,1,32]{2,1,0:T(1,128)S(1)}, ...), condition=%wide.region_4.5_spmd, body=%wide.region_3.4_spmd.sunk | while | flops 524294 | bytes 3146259 | solution.py:23
  400.4 1.4 bitcast_add_fusion.6
  401.9 1.4 bitcast_add_fusion.6
  403.4 1.4 bitcast_add_fusion.6
  404.9 1.4 bitcast_add_fusion.6
  406.4 1.4 bitcast_add_fusion.6
  407.9 1.4 bitcast_add_fusion.6
  409.4 1.4 bitcast_add_fusion.6
  410.9 1.4 bitcast_add_fusion.6
  412.4 1.4 bitcast_add_fusion.6
  413.9 1.4 bitcast_add_fusion.6
  415.4 1.4 bitcast_add_fusion.6
  416.9 1.4 bitcast_add_fusion.6
  418.4 1.4 bitcast_add_fusion.6
  419.8 1.4 bitcast_add_fusion.6
  436.3 1.4 bitcast_add_fusion.6
  445.3 1.4 bitcast_add_fusion.6
  446.7 1.6 multiply_reduce_fusion.2
  449.4 1.6 multiply_reduce_fusion.3
  452.4 1.9 convolution_bitcast_fusion.2
  455.5 4.6 fusion.31
  460.0 3.9 multiply_reduce_fusion.4
  463.9 1.8 convolution_bitcast_fusion.3
  466.2 420.2 %all-reduce = f32[4096]{0:T(1024)S(1)} all-reduce(f32[4096]{0:T(1024)S(1)} %dynamic-update-slice), channel_id=5, replica_groups=mesh['dp'=4,'ctx'=32,'tp'=4] {'dp','ctx'}, use_global_device_ids=true, to_apply=%add | all-reduce | flops 4096 | bytes 32768
  889.4 1.8 reduce_window_sum.22
  891.7 85.0 %reduce-scatter.3.cloned.1.call-done = f32[1,32,128]{2,1,0:T(8,128)} async-done(((f32[1,128,128]{2,1,0:T(8,128)}), f32[1,32,128]{2,1,0:T(8,128)}) %reduce-scatter.3.cloned.1.call-update) | async-done | bytes 16400 | tf_op jit(solution)/shard_map/reduce_scatter | solution.py:149
  (118 shorter events, 34.2 us)
Async XLA Ops:
  7.2 2.7 copy-start.8
  7.2 2.8 copy-start.13
  7.2 201.8 %all-gather.7.cloned.1.call-start = ((), (), s32[]{:S(2)}) async-start(), calls=%async_computation.4 | async-start | bytes 34603008 | tf_op jit(solution)/shard_map/all_gather | solution.py:14
  9.8 3.3 copy-start.4
  9.8 3.4 copy-start.10
  9.9 3.6 copy-start.9
  13.1 387.1 %all-gather.9.cloned.1.call-start = ((), (), s32[]{:S(2)}) async-start(), calls=%async_computation.5 | async-start | bytes 34603008 | tf_op jit(solution)/shard_map/all_gather | solution.py:14
  13.5 43.8 %copy-start.1 = (bf16[1,128,2048]{1,2,0:T(8,128)(2,1)}, bf16[1,128,2048]{1,2,0:T(8,128)(2,1)S(1)}, u32[]{:S(2)}) copy-start(bf16[1,128,2048]{1,2,0:T(8,128)(2,1)S(1)} %copy.84) | copy-start | bytes 1572868
  16.0 875.7 %reduce-scatter.5.cloned.1.call-start = ((), (), s32[]{:S(2)}) async-start(), calls=%async_computation.3 | async-start | bytes 81920 | tf_op jit(solution)/shard_map/reduce_scatter | solution.py:150
  446.7 1.6 copy-start
  448.3 1.0 copy-start.2
  449.4 1.7 copy-start.5
  451.1 4.3 copy-start.14
  455.2 521.5 %reduce-scatter.3.cloned.1.call-start = ((), (), s32[]{:S(2)}) async-start(), calls=%async_computation.2 | async-start | bytes 81920 | tf_op jit(solution)/shard_map/reduce_scatter | solution.py:149
  455.4 4.6 copy-start.3
  455.5 4.6 copy-start.7
  460.0 3.9 copy-start.6
  463.9 422.6 %copy-start.12 = (bf16[1,128,32,64]{1,3,2,0:T(8,128)(2,1)S(1)}, bf16[1,128,32,64]{1,3,2,0:T(8,128)(2,1)}, u32[]{:S(2)}) copy-start(bf16[1,128,32,64]{1,3,2,0:T(8,128)(2,1)} %get-tuple-element.248) | copy-start | bytes 1572868
  463.9 423.6 %copy-start.11 = (bf16[1,128,32,64]{1,3,2,0:T(8,128)(2,1)S(1)}, bf16[1,128,32,64]{1,3,2,0:T(8,128)(2,1)}, u32[]{:S(2)}) copy-start(bf16[1,128,32,64]{1,3,2,0:T(8,128)(2,1)} %fusion.31) | copy-start | bytes 1572868
Sparse Core Ops, SparseCore 0:
  13.3 195.7 all-gather.6
  211.1 189.0 all-gather.8
  455.3 19.0 reduce-scatter.4
  889.5 87.2 reduce-scatter.2
